TPU v7x, 512 devices: a whole 4x4x16 slice. The times are simulated.
512 devices in a mesh: row: 32 (over x, y, core), col: 16 (over z).
Axes of the slice: x: 4, y: 4, z: 16, core: 2. Of those that a mesh axis runs over, the one named last changes fastest.
Arguments:
- tokens: bfloat16 [4096, 2560], P('row', 'col'), may hold values from -6 to 6
- w_gate: bfloat16 [512, 192, 2560], P(('row', 'col')), may hold values from -0.125 to 0.125
- w_up: bfloat16 [512, 192, 2560], P(('row', 'col')), may hold values from -0.125 to 0.125
- w_down: bfloat16 [512, 192, 2560], P(('row', 'col')), may hold values from -0.15625 to 0.15625
- adp_down: bfloat16 [64, 16, 2560], P('row', None, 'col'), may hold values from -0.125 to 0.125
- adp_up: bfloat16 [64, 16, 2560], P('row', None, 'col'), may hold values from -1.5 to 1.5
- expert_ids: int32 [4096, 6], P('row'), may hold values from 0 to 63, all different within a row; in each aligned block of 128 rows (0 to 127, 128 to 255, ...) at most 16 rows name the same one
- gate_vals: float32 [4096, 6], P('row'), may hold values from 0.05 to 0.5
- lengths: int32 [16], replicated, may hold values from 1 to 1365, 4096 in all
- perm: int32 [4096], P('row'), may hold values from 0 to 4095, each once
- req_adapter: int32 [16], replicated, may hold values from 0 to 63
Outputs:
- layer_out: bfloat16 [4096, 2560], P('row', 'col')
Inputs may be any that keep to these rules, and one draw needn't show every extreme that they name: `expert_ids`: within the 128 rows of one index of row, no expert is named by more than 16 rows, a bound that some block reaches; each row names 6 different experts. `perm`: each position appears once. `lengths`: they sum to 4096; the longest is exactly 4096 // 3.
All inputs are finite; a program needn't handle non-finite values.
Results may differ from a plain program's by a relative error of at most 0.0051.
Values may be sent and summed in bfloat16 or wider, within the bound.
A program may use at most 128 MiB of HBM per device.

v0:
```python
import jax
import jax.numpy as jnp
from jax import lax
from jax.sharding import PartitionSpec as P

adapter_scale_factor = 2.0


def contract_last(left, right):
    return lax.dot_general(
        left, right, (((1,), (1,)), ((), ())), preferred_element_type=jnp.float32
    )


def body(
    tokens,
    w_gate,
    w_up,
    w_down,
    adp_down,
    adp_up,
    expert_ids,
    gate_vals,
    lengths,
    perm,
    req_adapter,
):
    count_tok = tokens.shape[0]
    share = tokens.shape[1]
    rows_count = lax.axis_size("row")
    cols_count = lax.axis_size("col")
    experts = 2 * rows_count
    parts = cols_count // 2
    which = lax.axis_index("col") // parts
    topk = expert_ids.shape[1]
    capacity = max(2, (4 * count_tok * topk + 3 * experts - 1) // (3 * experts))
    weight_gate = w_gate[0]
    weight_up = w_up[0]
    down_projection_weight = w_down[0]
    flat_ids = expert_ids.reshape(-1)
    onehot = (flat_ids[:, None] == jnp.arange(experts, dtype=jnp.int32)[None, :]).astype(jnp.int32)
    slot = jnp.sum(onehot * jnp.cumsum(onehot, axis=0), axis=1) - 1
    place = (flat_ids * capacity + slot).reshape(count_tok, topk)
    targets = jnp.arange(experts * capacity, dtype=jnp.int32)
    dispatch = jnp.any(targets[:, None, None] == place[None, :, :], axis=2).astype(jnp.bfloat16)
    combine = jnp.sum(
        jnp.where(
            place[:, :, None] == targets[None, None, :], gate_vals[:, :, None], jnp.float32(0.0)
        ),
        axis=1,
    )
    outgoing = jnp.dot(dispatch, tokens, preferred_element_type=jnp.float32).astype(jnp.bfloat16)
    outgoing = outgoing.reshape(rows_count, 2, capacity, share)
    arrival_rows = lax.all_to_all(outgoing, "row", split_axis=0, concat_axis=0, tiled=True)
    piece = lax.all_gather(arrival_rows, "col", axis=3, tiled=True)
    cols = piece.shape[3]
    mine = lax.dynamic_index_in_dim(piece, which, 1, keepdims=False).reshape(
        rows_count * capacity, cols
    )
    gate = contract_last(mine, weight_gate)
    upper = contract_last(mine, weight_up)
    hidden = (jax.nn.silu(gate) * upper).astype(jnp.bfloat16)
    partial_out = jnp.dot(
        hidden, down_projection_weight, preferred_element_type=jnp.float32
    ).astype(jnp.bfloat16)
    pieces = partial_out.reshape(rows_count * capacity, cols_count, share)
    received = lax.all_to_all(pieces, "col", split_axis=1, concat_axis=1, tiled=True)
    summed = jnp.sum(
        received.astype(jnp.float32).reshape(rows_count, capacity, 2, parts, share), axis=3
    )
    summed = summed.transpose(0, 2, 1, 3)
    returned = lax.all_to_all(summed, "row", split_axis=0, concat_axis=0, tiled=True)
    dispatched_tokens = jnp.dot(
        combine, returned.reshape(experts * capacity, share), precision=lax.Precision.HIGHEST
    )
    down_all, up_all = (
        lax.all_gather(adp_down, "row", axis=0, tiled=True),
        lax.all_gather(adp_up, "row", axis=0, tiled=True),
    )
    adapters = down_all.shape[0]
    rank = down_all.shape[1]
    nreq = lengths.shape[0]
    ends = jnp.cumsum(lengths)
    request = jnp.sum((perm[:, None] >= ends[None, :]).astype(jnp.int32), axis=1)
    adapter = jnp.sum(
        jnp.where(
            request[:, None] == jnp.arange(nreq, dtype=jnp.int32)[None, :], req_adapter[None, :], 0
        ),
        axis=1,
    )
    onehot_a = (adapter[:, None] == jnp.arange(adapters, dtype=jnp.int32)[None, :]).astype(
        jnp.float32
    )
    projected = jnp.einsum(
        "td,kd->tk",
        tokens,
        down_all.reshape(adapters * rank, share),
        preferred_element_type=jnp.float32,
    )
    partial_low = jnp.sum(
        projected.reshape(count_tok, adapters, rank) * onehot_a[:, :, None], axis=1
    )
    low = lax.psum(partial_low, "col").astype(jnp.bfloat16)
    expanded = (onehot_a.astype(jnp.bfloat16)[:, :, None] * low[:, None, :]).reshape(
        count_tok, adapters * rank
    )
    adapter_update = jnp.dot(
        expanded, up_all.reshape(adapters * rank, share), preferred_element_type=jnp.float32
    )
    return (dispatched_tokens + adapter_scale_factor * adapter_update).astype(jnp.bfloat16)


def solution(mesh):
    in_specs = (
        P("row", "col"),
        P(("row", "col"), None, None),
        P(("row", "col"), None, None),
        P(("row", "col"), None, None),
        P("row", None, "col"),
        P("row", None, "col"),
        P("row", None),
        P("row", None),
        P(),
        P("row"),
        P(),
    )
    out_specs = P("row", "col")
    return jax.shard_map(body, mesh=mesh, in_specs=in_specs, out_specs=out_specs, check_vma=False)
```

profile of v0, /device:TPU:1, one launch (start us, length us, event | category | flops | bytes accessed | tf_op | source)
XLA Modules:
  0.0 505.6 jit_solution(4456110021463680649)
XLA Ops:
  6.5 0.0 copy-start
  6.5 0.0 all-gather.2.cloned.1.call-start
  6.5 0.9 copy.72
  7.4 0.1 eq.88
  7.6 0.1 eq.84
  7.7 1.8 reduce-window.18
  9.5 0.3 slice_reduce_fusion
  9.8 0.1 fusion.20
  10.0 0.1 sub.11
  10.1 0.1 copy.75
  10.2 0.7 multiply_add_fusion
  10.9 0.5 fusion
  11.4 1.0 convolution_convert_fusion.1
  12.4 0.2 copy.76
  12.6 21.3 %all_to_all.15 = bf16[32,2,16,160]{3,2,1,0:T(8,128)(2,1)S(1)} all-to-all(bf16[32,2,16,160]{3,2,1,0:T(8,128)(2,1)S(1)} %bitcast.59), channel_id=1, replica_groups=mesh['row'=32,'col'=16] {'row'}, dimensions={0} | all-to-all | bytes 655360 | tf_op jit(solution)/shard_map/all_to_all | solution.py:54
  33.9 2.3 copy.77
  36.2 0.0 all-gather.2.cloned.1.call-update
  36.2 231.6 %all-gather.2.cloned.1.call-done = bf16[32,2,16,2560]{0,2,1,3:T(8,128)(2,1)} async-done(((bf16[32,2,16,160]{0,2,1,3:T(8,128)(2,1)}), bf16[32,2,16,2560]{0,2,1,3:T(8,128)(2,1)}) %all-gather.2.cloned.1.call-update) | async-done | bytes 5242896 | tf_op jit(solution)/shard_map/all_gather | solution.py:55
  267.8 10.4 %constant_dynamic-slice_fusion = bf16[32,1,16,2560]{0,2,1,3:T(8,128)(2,1)} fusion(bf16[32,2,16,2560]{0,2,1,3:T(8,128)(2,1)} %all-gather.2.cloned.1.call-done, s32[]{:T(128)S(6)} %select_n.19), kind=kLoop, calls=%fused_computation.47 | loop fusion | bytes 5242884 | tf_op jit(solution)/shard_map/jit(dynamic_index_in_dim)/dynamic_slice | solution.py:57
  278.2 13.0 %copy.86 = bf16[32,1,16,2560]{3,2,0,1:T(8,128)(2,1)} copy(bf16[32,1,16,2560]{0,2,1,3:T(8,128)(2,1)} %constant_dynamic-slice_fusion) | data formatting | bytes 5242880
  291.2 2.8 fusion.9
  294.0 0.0 copy-done
  294.0 0.0 copy-done.7
  294.1 5.2 %convolution_convert_fusion = bf16[512,2560]{1,0:T(8,128)(2,1)} fusion(bf16[512,2560]{1,0:T(8,128)(2,1)} %bitcast.58, bf16[1,192,2560]{2,1,0:T(8,128)(2,1)S(1)} %copy-done, bf16[1,192,2560]{2,1,0:T(8,128)(2,1)S(1)} %copy-done.7, f32[512,192]{0,1:T(8,128)S(1)} %fusion.9), kind=kOutput, calls=%fused_computation.1 | convolution fusion | flops 1008533504 | bytes 7602176 | tf_op jit(solution)/shard_map/dot_general | solution.py:63
  299.2 4.4 copy.79
  303.6 8.8 %all-to-all-start.1 = ((bf16[512,16,160]{0,2,1:T(8,128)(2,1)}), bf16[512,16,160]{0,2,1:T(8,128)(2,1)}, u32[]{:S(2)}, u32[]{:S(2)}) async-start(bf16[512,16,160]{0,2,1:T(8,128)(2,1)} %bitcast.55), calls=%async_computation.1 | async-start | bytes 5242880 | tf_op jit(solution)/shard_map/all_to_all | solution.py:67
  312.4 0.1 copy.82
  312.5 0.1 reduce.2
  312.6 0.0 copy-done.2
  312.7 25.6 %all_gather.10 = bf16[64,16,160]{2,1,0:T(8,128)(2,1)S(1)} all-gather(bf16[2,16,160]{2,1,0:T(8,128)(2,1)S(1)} %copy-done.2), channel_id=1, replica_groups=mesh['row'=32,'col'=16] {'row'}, dimensions={0}, use_global_device_ids=true | all-gather | bytes 337920 | tf_op jit(solution)/shard_map/all_gather | solution.py:77
  338.2 0.1 convert_reduce_fusion.1
  338.3 0.1 select_reduce_fusion.1
  338.4 88.4 %all-to-all-done.1 = bf16[512,16,160]{0,2,1:T(8,128)(2,1)} async-done(((bf16[512,16,160]{0,2,1:T(8,128)(2,1)}), bf16[512,16,160]{0,2,1:T(8,128)(2,1)}, u32[]{:S(2)}, u32[]{:S(2)}) %all-to-all-start.1) | async-done | bytes 2621472 | tf_op jit(solution)/shard_map/all_to_all | solution.py:67
  426.8 2.2 convert_reduce_fusion
  428.9 0.0 copy-start.1
  429.0 0.0 copy-start.3
  429.0 0.0 copy-start.4
  429.0 1.3 copy.85
  430.3 11.3 %all-to-all-start.2 = ((f32[32,2,16,160]{3,1,2,0:T(2,128)}), f32[32,2,16,160]{3,1,2,0:T(2,128)S(1)}, u32[]{:S(2)}, u32[]{:S(2)}) async-start(f32[32,2,16,160]{3,1,2,0:T(2,128)} %bitcast.10), calls=%async_computation.2 | async-start | bytes 2097152 | tf_op jit(solution)/shard_map/all_to_all | solution.py:72
  441.6 0.3 fusion.2
  441.9 22.3 %psum.7 = bf16[128,16]{0,1:T(8,128)(2,1)S(1)} all-reduce(f32[128,16]{0,1:T(8,128)S(1)} %fusion.2), channel_id=1, replica_groups=mesh['row'=32,'col'=16] {'col'}, use_global_device_ids=true, to_apply=%region_10.11 | all-reduce | flops 2048 | bytes 12288 | tf_op jit(solution)/shard_map/psum | solution.py:103
  464.2 31.2 %all_gather.11 = bf16[64,16,160]{2,1,0:T(8,128)(2,1)S(1)} all-gather(bf16[2,16,160]{2,1,0:T(8,128)(2,1)S(1)} %copy-done.3), channel_id=1, replica_groups=mesh['row'=32,'col'=16] {'row'}, dimensions={0}, use_global_device_ids=true | all-gather | bytes 337920 | tf_op jit(solution)/shard_map/all_gather | solution.py:78
  495.4 0.0 copy-done.4
  495.5 0.4 select_reduce_fusion
  495.9 0.0 all-to-all-done.2
  495.9 0.1 copy.81
  496.0 1.8 fusion.29
  497.8 1.0 fusion.5
  (17 shorter events, 0.1 us)
Async XLA Ops:
  6.5 287.5 %copy-start = (bf16[1,192,2560]{2,1,0:T(8,128)(2,1)S(1)}, bf16[1,192,2560]{2,1,0:T(8,128)(2,1)}, u32[]{:S(2)}) copy-start(bf16[1,192,2560]{2,1,0:T(8,128)(2,1)} %param.14) | copy-start | bytes 2949124
  6.5 261.2 %all-gather.2.cloned.1.call-start = ((), (), s32[]{:S(2)}) async-start(), calls=%async_computation.3 | async-start | bytes 22282240 | tf_op jit(solution)/shard_map/all_gather | solution.py:55
  278.2 13.1 %copy-start.6 = (bf16[1,192,2560]{2,1,0:T(8,128)(2,1)S(1)}, bf16[1,192,2560]{2,1,0:T(8,128)(2,1)}, u32[]{:S(2)}) copy-start(bf16[1,192,2560]{2,1,0:T(8,128)(2,1)} %param.12) | copy-start | bytes 2949124
  291.2 2.8 copy-start.7
  303.6 8.8 %copy-start.5 = (s32[16]{0:T(128)S(1)}, s32[16]{0:T(128)}, u32[]{:S(2)}) copy-start(s32[16]{0:T(128)} %param.19) | copy-start | bytes 196
  303.6 9.0 %copy-start.2 = (bf16[2,16,160]{2,1,0:T(8,128)(2,1)S(1)}, bf16[2,16,160]{2,1,0:T(8,128)(2,1)}, u32[]{:S(2)}) copy-start(bf16[2,16,160]{2,1,0:T(8,128)(2,1)} %param.15) | copy-start | bytes 30724
  303.6 34.6 %copy-start.8 = (s32[128]{0:T(128)S(1)}, s32[128]{0:T(128)}, u32[]{:S(2)}) copy-start(s32[128]{0:T(128)} %param.20) | copy-start | bytes 1540
  303.6 34.7 %copy-start.9 = (s32[16]{0:T(128)S(1)}, s32[16]{0:T(128)}, u32[]{:S(2)}) copy-start(s32[16]{0:T(128)} %param.21) | copy-start | bytes 196
  303.6 123.2 %all-to-all-start.1 = ((bf16[512,16,160]{0,2,1:T(8,128)(2,1)}), bf16[512,16,160]{0,2,1:T(8,128)(2,1)}, u32[]{:S(2)}, u32[]{:S(2)}) async-start(bf16[512,16,160]{0,2,1:T(8,128)(2,1)} %bitcast.55), calls=%async_computation.1 | async-start | bytes 5242880 | tf_op jit(solution)/shard_map/all_to_all | solution.py:67
  428.9 12.6 %copy-start.1 = (bf16[128,160]{0,1:T(8,128)(2,1)S(1)}, bf16[128,160]{0,1:T(8,128)(2,1)}, u32[]{:S(2)}) copy-start(bf16[128,160]{0,1:T(8,128)(2,1)} %param.11) | copy-start | bytes 122884
  429.0 35.3 %copy-start.3 = (bf16[2,16,160]{2,1,0:T(8,128)(2,1)S(1)}, bf16[2,16,160]{2,1,0:T(8,128)(2,1)}, u32[]{:S(2)}) copy-start(bf16[2,16,160]{2,1,0:T(8,128)(2,1)} %param.16) | copy-start | bytes 30724
  429.0 66.5 %copy-start.4 = (f32[128,6]{0,1:T(8,128)S(1)}, f32[128,6]{0,1:T(8,128)}, u32[]{:S(2)}) copy-start(f32[128,6]{0,1:T(8,128)} %param.18) | copy-start | bytes 9220
  430.3 65.6 %all-to-all-start.2 = ((f32[32,2,16,160]{3,1,2,0:T(2,128)}), f32[32,2,16,160]{3,1,2,0:T(2,128)S(1)}, u32[]{:S(2)}, u32[]{:S(2)}) async-start(f32[32,2,16,160]{3,1,2,0:T(2,128)} %bitcast.10), calls=%async_computation.2 | async-start | bytes 2097152 | tf_op jit(solution)/shard_map/all_to_all | solution.py:72
Sparse Core Ops, SparseCore 0:
  36.3 231.4 all-gather.1
where the time goes:
time: 507 us; the launch traced here: 506 us
  waiting for transfers between devices  320 us (63%)
  blocking collectives  100 us (20%)
  local copies, waits for them, and re-layouts  33.4 us (7%)
  starting transfers between devices  20 us (4%)
  between operations  13.6 us (3%)
  matrix products  12.1 us (2%)
  other arithmetic  6.11 us (1%)
    all_gather x1, waiting for transfers between devices, body(): piece = lax.all_gather(arrival_rows, 'col', axis=3, tiled=True)  232 us
    all_to_all x1, waiting for transfers between devices, body(): lax.all_to_all(pieces, 'col', split_axis=1, concat_axis=1, tiled=True)  88.4 us
    all_gather x1, blocking collectives, body(): lax.all_gather(adp_up, 'row', axis=0, tiled=True)  31.2 us
    all_gather x1, blocking collectives, body(): lax.all_gather(adp_down, 'row', axis=0, tiled=True)  25.6 us
    psum x1, blocking collectives, body(): low = lax.psum(partial_low, 'col').astype(jnp.bfloat16)  22.3 us
    all_to_all x1, blocking collectives, body(): lax.all_to_all(outgoing, 'row', split_axis=0, concat_axis=0, tiled=True)  21.3 us
    unnamed x23, local copies, waits for them, and re-layouts  15.3 us
    all_to_all x1, starting transfers between devices, body(): lax.all_to_all(summed, 'row', split_axis=0, concat_axis=0, tiled=True)  11.3 us
  transfers between devices with their start and end apart: 3, of which 2 were waited for; matrix products, arithmetic and copies ran while one was open for 0% of the time, Pallas kernels for 0%

commit v1 on v0

--- a/solution.py
+++ b/solution.py
@@ -100,7 +100,7 @@
     partial_low = jnp.sum(
         projected.reshape(count_tok, adapters, rank) * onehot_a[:, :, None], axis=1
     )
-    low = lax.psum(partial_low, "col").astype(jnp.bfloat16)
+    low = jnp.sum(lax.all_gather(partial_low, "col"), axis=0).astype(jnp.bfloat16)
     expanded = (onehot_a.astype(jnp.bfloat16)[:, :, None] * low[:, None, :]).reshape(
         count_tok, adapters * rank
     )

time: 507 us -> 537 us (1.059)
  waiting for transfers between devices: 320 us -> 346 us
    all_to_all x1, waiting for transfers between devices: 88.4 us -> 114 us  [body(): lax.all_to_all(pieces, 'col', split_axis=1, concat_axis=1, tiled=True)]
    psum x1 -> x0, blocking collectives: 22.3 us -> none  [body(): low = lax.psum(partial_low, 'col').astype(jnp.bfloat16)]
    all_gather x0 -> x1, blocking collectives: none -> 20.5 us  [body(): lax.all_gather(partial_low, 'col')]
    all_gather x1, blocking collectives: 25.6 us -> 33.4 us  [body(): lax.all_gather(adp_down, 'row', axis=0, tiled=True)]
    unnamed x23 -> x24, local copies, waits for them, and re-layouts: 15.3 us -> 15.3 us
where the time goes in v1:
time: 537 us; the launch traced here: 536 us
  waiting for transfers between devices  346 us (64%)
  blocking collectives  105 us (20%)
  local copies, waits for them, and re-layouts  33.5 us (6%)
  starting transfers between devices  20.2 us (4%)
  between operations  13.6 us (3%)
  matrix products  12.1 us (2%)
  other arithmetic  6.14 us (1%)
    all_gather x1, waiting for transfers between devices, body(): piece = lax.all_gather(arrival_rows, 'col', axis=3, tiled=True)  232 us
    all_to_all x1, waiting for transfers between devices, body(): lax.all_to_all(pieces, 'col', split_axis=1, concat_axis=1, tiled=True)  114 us
    all_gather x1, blocking collectives, body(): lax.all_gather(adp_down, 'row', axis=0, tiled=True)  33.4 us
    all_gather x1, blocking collectives, body(): lax.all_gather(adp_up, 'row', axis=0, tiled=True)  29.9 us
    all_to_all x1, blocking collectives, body(): lax.all_to_all(outgoing, 'row', split_axis=0, concat_axis=0, tiled=True)  21.3 us
    all_gather x1, blocking collectives, body(): lax.all_gather(partial_low, 'col')  20.5 us
    unnamed x24, local copies, waits for them, and re-layouts  15.3 us
    all_to_all x1, starting transfers between devices, body(): lax.all_to_all(summed, 'row', split_axis=0, concat_axis=0, tiled=True)  11.4 us
  transfers between devices with their start and end apart: 3, of which 2 were waited for; matrix products, arithmetic and copies ran while one was open for 0% of the time, Pallas kernels for 0%

profile of v1, /device:TPU:1, one launch (start us, length us, event | category | flops | bytes accessed | tf_op | source)
XLA Modules:
  0.0 536.1 jit_solution(4074852227479328554)
XLA Ops:
  6.5 0.0 copy-start
  6.5 0.0 all-gather.3.cloned.1.call-start
  6.5 0.9 copy.72
  7.4 0.1 eq.88
  7.6 0.1 eq.84
  7.7 1.8 reduce-window.18
  9.5 0.3 slice_reduce_fusion
  9.8 0.1 fusion.20
  10.0 0.1 sub.11
  10.1 0.1 copy.75
  10.2 0.7 multiply_add_fusion
  10.9 0.5 fusion
  11.4 1.0 convolution_convert_fusion.1
  12.4 0.2 copy.76
  12.6 21.3 %all_to_all.15 = bf16[32,2,16,160]{3,2,1,0:T(8,128)(2,1)S(1)} all-to-all(bf16[32,2,16,160]{3,2,1,0:T(8,128)(2,1)S(1)} %bitcast.64), channel_id=1, replica_groups=mesh['row'=32,'col'=16] {'row'}, dimensions={0} | all-to-all | bytes 655360 | tf_op jit(solution)/shard_map/all_to_all | solution.py:54
  33.9 2.3 copy.77
  36.2 0.0 all-gather.3.cloned.1.call-update
  36.2 231.6 %all-gather.3.cloned.1.call-done = bf16[32,2,16,2560]{0,2,1,3:T(8,128)(2,1)} async-done(((bf16[32,2,16,160]{0,2,1,3:T(8,128)(2,1)}), bf16[32,2,16,2560]{0,2,1,3:T(8,128)(2,1)}) %all-gather.3.cloned.1.call-update) | async-done | bytes 5242896 | tf_op jit(solution)/shard_map/all_gather | solution.py:55
  267.8 10.4 %constant_dynamic-slice_fusion = bf16[32,1,16,2560]{0,2,1,3:T(8,128)(2,1)} fusion(bf16[32,2,16,2560]{0,2,1,3:T(8,128)(2,1)} %all-gather.3.cloned.1.call-done, s32[]{:T(128)S(6)} %select_n.19), kind=kLoop, calls=%fused_computation.48 | loop fusion | bytes 5242884 | tf_op jit(solution)/shard_map/jit(dynamic_index_in_dim)/dynamic_slice | solution.py:57
  278.2 13.0 %copy.86 = bf16[32,1,16,2560]{3,2,0,1:T(8,128)(2,1)} copy(bf16[32,1,16,2560]{0,2,1,3:T(8,128)(2,1)} %constant_dynamic-slice_fusion) | data formatting | bytes 5242880
  291.2 0.0 copy-done.6
  291.2 2.8 fusion.9
  294.0 0.0 copy-done
  294.0 0.0 copy-done.7
  294.1 5.2 convolution_convert_fusion
  299.2 4.4 copy.79
  303.6 8.8 %all-to-all-start.1 = ((bf16[512,16,160]{0,2,1:T(8,128)(2,1)}), bf16[512,16,160]{0,2,1:T(8,128)(2,1)}, u32[]{:S(2)}, u32[]{:S(2)}) async-start(bf16[512,16,160]{0,2,1:T(8,128)(2,1)} %bitcast.60), calls=%async_computation.1 | async-start | bytes 5242880 | tf_op jit(solution)/shard_map/all_to_all | solution.py:67
  312.4 0.1 copy.82
  312.5 0.1 reduce.2
  312.6 0.1 convert_reduce_fusion.1
  312.7 0.0 copy-done.9
  312.7 0.1 select_reduce_fusion.1
  312.8 113.9 %all-to-all-done.1 = bf16[512,16,160]{0,2,1:T(8,128)(2,1)} async-done(((bf16[512,16,160]{0,2,1:T(8,128)(2,1)}), bf16[512,16,160]{0,2,1:T(8,128)(2,1)}, u32[]{:S(2)}, u32[]{:S(2)}) %all-to-all-start.1) | async-done | bytes 2621472 | tf_op jit(solution)/shard_map/all_to_all | solution.py:67
  426.8 2.2 convert_reduce_fusion
  428.9 0.0 copy-start.2
  428.9 0.0 copy-start.1
  429.0 0.0 copy-start.3
  429.0 1.3 copy.85
  430.3 11.4 %all-to-all-start.2 = ((f32[32,2,16,160]{3,1,2,0:T(2,128)}), f32[32,2,16,160]{3,1,2,0:T(2,128)S(1)}, u32[]{:S(2)}, u32[]{:S(2)}) async-start(f32[32,2,16,160]{3,1,2,0:T(2,128)} %bitcast.10), calls=%async_computation.2 | async-start | bytes 2097152 | tf_op jit(solution)/shard_map/all_to_all | solution.py:72
  441.7 33.4 %all_gather.16 = bf16[64,16,160]{2,1,0:T(8,128)(2,1)S(1)} all-gather(bf16[2,16,160]{2,1,0:T(8,128)(2,1)S(1)} %copy-done.2), channel_id=1, replica_groups=mesh['row'=32,'col'=16] {'row'}, dimensions={0}, use_global_device_ids=true | all-gather | bytes 337920 | tf_op jit(solution)/shard_map/all_gather | solution.py:77
  475.1 0.3 fusion.2
  475.5 20.5 %all-gather = f32[2048,16]{0,1:T(8,128)S(1)} all-gather(f32[128,16]{0,1:T(8,128)S(1)} %fusion.2), channel_id=2, replica_groups=mesh['row'=32,'col'=16] {'col'}, dimensions={0}, use_global_device_ids=true | all-gather | bytes 139264 | tf_op jit(solution)/shard_map/all_gather | solution.py:103
  496.0 29.9 %all_gather.19 = bf16[64,16,160]{2,1,0:T(8,128)(2,1)S(1)} all-gather(bf16[2,16,160]{2,1,0:T(8,128)(2,1)S(1)} %copy-done.3), channel_id=1, replica_groups=mesh['row'=32,'col'=16] {'row'}, dimensions={0}, use_global_device_ids=true | all-gather | bytes 337920 | tf_op jit(solution)/shard_map/all_gather | solution.py:78
  525.9 0.4 select_reduce_fusion
  526.4 0.0 all-to-all-done.2
  526.4 0.1 copy.81
  526.5 1.8 fusion.29
  528.3 1.0 fusion.5
  (19 shorter events, 0.2 us)
Async XLA Ops:
  6.5 287.5 %copy-start = (bf16[1,192,2560]{2,1,0:T(8,128)(2,1)S(1)}, bf16[1,192,2560]{2,1,0:T(8,128)(2,1)}, u32[]{:S(2)}) copy-start(bf16[1,192,2560]{2,1,0:T(8,128)(2,1)} %param.14) | copy-start | bytes 2949124
  6.5 261.2 %all-gather.3.cloned.1.call-start = ((), (), s32[]{:S(2)}) async-start(), calls=%async_computation.3 | async-start | bytes 22282240 | tf_op jit(solution)/shard_map/all_gather | solution.py:55
  278.2 13.1 %copy-start.6 = (bf16[1,192,2560]{2,1,0:T(8,128)(2,1)S(1)}, bf16[1,192,2560]{2,1,0:T(8,128)(2,1)}, u32[]{:S(2)}) copy-start(bf16[1,192,2560]{2,1,0:T(8,128)(2,1)} %param.12) | copy-start | bytes 2949124
  291.2 2.8 copy-start.7
  303.6 8.8 %copy-start.5 = (s32[16]{0:T(128)S(1)}, s32[16]{0:T(128)}, u32[]{:S(2)}) copy-start(s32[16]{0:T(128)} %param.19) | copy-start | bytes 196
  303.6 9.0 %copy-start.8 = (s32[128]{0:T(128)S(1)}, s32[128]{0:T(128)}, u32[]{:S(2)}) copy-start(s32[128]{0:T(128)} %param.20) | copy-start | bytes 1540
  303.6 9.1 %copy-start.9 = (s32[16]{0:T(128)S(1)}, s32[16]{0:T(128)}, u32[]{:S(2)}) copy-start(s32[16]{0:T(128)} %param.21) | copy-start | bytes 196
  303.6 123.2 %all-to-all-start.1 = ((bf16[512,16,160]{0,2,1:T(8,128)(2,1)}), bf16[512,16,160]{0,2,1:T(8,128)(2,1)}, u32[]{:S(2)}, u32[]{:S(2)}) async-start(bf16[512,16,160]{0,2,1:T(8,128)(2,1)} %bitcast.60), calls=%async_computation.1 | async-start | bytes 5242880 | tf_op jit(solution)/shard_map/all_to_all | solution.py:67
  428.9 12.7 %copy-start.2 = (bf16[2,16,160]{2,1,0:T(8,128)(2,1)S(1)}, bf16[2,16,160]{2,1,0:T(8,128)(2,1)}, u32[]{:S(2)}) copy-start(bf16[2,16,160]{2,1,0:T(8,128)(2,1)} %param.15) | copy-start | bytes 30724
  428.9 46.2 %copy-start.1 = (bf16[128,160]{0,1:T(8,128)(2,1)S(1)}, bf16[128,160]{0,1:T(8,128)(2,1)}, u32[]{:S(2)}) copy-start(bf16[128,160]{0,1:T(8,128)(2,1)} %param.11) | copy-start | bytes 122884
  429.0 67.1 %copy-start.3 = (bf16[2,16,160]{2,1,0:T(8,128)(2,1)S(1)}, bf16[2,16,160]{2,1,0:T(8,128)(2,1)}, u32[]{:S(2)}) copy-start(bf16[2,16,160]{2,1,0:T(8,128)(2,1)} %param.16) | copy-start | bytes 30724
  430.3 95.7 %copy-start.4 = (f32[128,6]{0,1:T(8,128)S(1)}, f32[128,6]{0,1:T(8,128)}, u32[]{:S(2)}) copy-start(f32[128,6]{0,1:T(8,128)} %param.18) | copy-start | bytes 9220
  430.3 96.1 %all-to-all-start.2 = ((f32[32,2,16,160]{3,1,2,0:T(2,128)}), f32[32,2,16,160]{3,1,2,0:T(2,128)S(1)}, u32[]{:S(2)}, u32[]{:S(2)}) async-start(f32[32,2,16,160]{3,1,2,0:T(2,128)} %bitcast.10), calls=%async_computation.2 | async-start | bytes 2097152 | tf_op jit(solution)/shard_map/all_to_all | solution.py:72
Sparse Core Ops, SparseCore 0:
  36.3 231.4 all-gather.2
